TPU v7x, 32 devices: a whole 2x2x4 slice. The times are simulated.
32 devices in a mesh: ctx: 8 (over y, x, core), ch: 4 (over z).
Axes of the slice: x: 2, y: 2, z: 4, core: 2. Of those that a mesh axis runs over, the one named last changes fastest.
Arguments:
- queries: bfloat16 [8192, 2048], P('ch', 'ctx'), may hold values from -6 to 6
- keys: bfloat16 [8192, 2048], P('ch', 'ctx'), may hold values from -6 to 6
- values: bfloat16 [8192, 2048], P('ch', 'ctx'), may hold values from -6 to 6
- short_taps: float32 [3, 7, 8192], P(None, None, 'ch'), may hold values from -2 to 2
- long_filter: bfloat16 [4, 2048, 2048], P('ch', 'ctx'), may hold values from -1.5 to 1.5
- skip_gain: float32 [4, 2048], P('ch', 'ctx'), may hold values from 0.5 to 1.5
Outputs:
- mixed: bfloat16 [8192, 2048], P('ch', 'ctx')
All inputs are finite; a program needn't handle non-finite values.
Results may differ from a plain program's by a relative error of at most 0.01.
Values may be sent and summed in bfloat16 or wider, within the bound.
A program may use at most 64 MiB of HBM per device.

v0:
```python
import math
import jax
import jax.numpy as jnp
from jax import lax
from jax.sharding import PartitionSpec as P

HIGH = lax.Precision.HIGHEST


def passed_along(value, axis, by):
    peers = lax.axis_size(axis)
    pairs = [(i, i + by) for i in range(peers) if 0 <= i + by < peers]
    return lax.ppermute(value, axis, pairs)


def short_conv(extended, taps, length):
    rim = taps.shape[0] - 1
    total = jnp.zeros((extended.shape[0], length), jnp.float32)
    for shift_j in range(taps.shape[0]):
        total = total + taps[shift_j][:, None] * extended[:, rim - shift_j : rim - shift_j + length]
    return total


def split_table(table):
    table_head = table.astype(jnp.bfloat16)
    table_rest = (table - table_head.astype(jnp.float32)).astype(jnp.bfloat16)
    return (table_head, table_rest)


def long_conv(gated, filters, skips):
    channels, length = gated.shape
    size = 2 * length
    cols = 128
    rows = size // cols
    half = rows // 2
    two_pi = 2.0 * math.pi
    row_idx = jnp.arange(rows, dtype=jnp.int32)
    half_idx = jnp.arange(half, dtype=jnp.int32)
    col_idx = jnp.arange(cols, dtype=jnp.int32)
    angle_rows = two_pi * (row_idx[:, None] * half_idx[None, :] % rows).astype(jnp.float32) / rows
    cos_rows, sin_rows = (jnp.cos(angle_rows), jnp.sin(angle_rows))
    cos_head, cos_rest = split_table(cos_rows)
    sin_head, sin_rest = split_table(sin_rows)
    angle_twist = two_pi * (row_idx[:, None] * col_idx[None, :]).astype(jnp.float32) / size
    cos_twist, sin_twist = (jnp.cos(angle_twist), jnp.sin(angle_twist))
    angle_cols = two_pi * (col_idx[:, None] * col_idx[None, :] % cols).astype(jnp.float32) / cols
    cos_cols, sin_cols = (jnp.cos(angle_cols), jnp.sin(angle_cols))

    def first_section(table_head, table_rest, shaped):
        return jnp.einsum(
            "ka,cab->ckb", table_head, shaped, preferred_element_type=jnp.float32
        ) + jnp.einsum("ka,cab->ckb", table_rest, shaped, preferred_element_type=jnp.float32)

    def forward(signal):
        blocks = signal.shape[0]
        shaped = signal.reshape(blocks, half, cols)
        first_re = first_section(cos_head, cos_rest, shaped)
        first_im = -first_section(sin_head, sin_rest, shaped)
        twist_re = first_re * cos_twist + first_im * sin_twist
        twist_im = first_im * cos_twist - first_re * sin_twist
        out_re = jnp.einsum("ckb,bm->ckm", twist_re, cos_cols, precision=HIGH) + jnp.einsum(
            "ckb,bm->ckm", twist_im, sin_cols, precision=HIGH
        )
        out_im = jnp.einsum("ckb,bm->ckm", twist_im, cos_cols, precision=HIGH) - jnp.einsum(
            "ckb,bm->ckm", twist_re, sin_cols, precision=HIGH
        )
        return (out_re, out_im)

    def inverse(spec_re, spec_im):
        blocks = spec_re.shape[0]
        back_re = jnp.einsum("ckm,mb->ckb", spec_re, cos_cols, precision=HIGH) - jnp.einsum(
            "ckm,mb->ckb", spec_im, sin_cols, precision=HIGH
        )
        back_im = jnp.einsum("ckm,mb->ckb", spec_im, cos_cols, precision=HIGH) + jnp.einsum(
            "ckm,mb->ckb", spec_re, sin_cols, precision=HIGH
        )
        turn_re = back_re * cos_twist - back_im * sin_twist
        turn_im = back_re * sin_twist + back_im * cos_twist
        result = jnp.einsum("ka,ckb->cab", cos_rows, turn_re, precision=HIGH) - jnp.einsum(
            "ka,ckb->cab", sin_rows, turn_im, precision=HIGH
        )
        return (result / size).reshape(blocks, length)

    block = math.gcd(channels, 16)
    count = channels // block

    def one_block(triple):
        sig, filt, gain = triple
        sig_re, sig_im = forward(sig)
        filt_re, filt_im = forward(filt)
        prod_re = sig_re * filt_re - sig_im * filt_im
        prod_im = sig_re * filt_im + sig_im * filt_re
        return inverse(prod_re, prod_im) + gain[:, None] * sig.astype(jnp.float32)

    outcome = lax.map(
        one_block,
        (
            gated.reshape(count, block, length),
            filters.reshape(count, block, length),
            skips.reshape(count, block),
        ),
    )
    return outcome.reshape(channels, length).astype(jnp.bfloat16)


def gate_product(first, second):
    return (first.astype(jnp.float32) * second.astype(jnp.float32)).astype(jnp.bfloat16)


def local(queries, keys, values, short_taps, long_filter, skip_gain):
    width, tok_local = queries.shape
    rim = short_taps.shape[1] - 1
    stacked = jnp.stack(
        [queries[:, tok_local - rim :], keys[:, tok_local - rim :], values[:, tok_local - rim :]]
    )
    before = passed_along(stacked, "ctx", 1)

    def extend_home(source, which):
        return jnp.concatenate([before[which], source], axis=1).astype(jnp.float32)

    q_short = short_conv(extend_home(queries, 0), short_taps[0], tok_local).astype(jnp.bfloat16)
    gated = (
        short_conv(extend_home(keys, 1), short_taps[1], tok_local)
        * short_conv(extend_home(values, 2), short_taps[2], tok_local)
    ).astype(jnp.bfloat16)
    g_owned = lax.all_to_all(gated, "ctx", split_axis=0, concat_axis=1, tiled=True)
    outgoing = long_conv(g_owned, long_filter[0], skip_gain[0])
    returned = lax.all_to_all(outgoing, "ctx", split_axis=1, concat_axis=0, tiled=True)
    return gate_product(q_short, returned)


def solution(mesh):
    placed = (
        P("ch", "ctx"),
        P("ch", "ctx"),
        P("ch", "ctx"),
        P(None, None, "ch"),
        P("ch", "ctx", None),
        P("ch", "ctx"),
    )
    return jax.shard_map(
        local, mesh=mesh, in_specs=placed, out_specs=P("ch", "ctx"), check_vma=False
    )
```

profile of v0, /device:TPU:0, one launch (start us, length us, event | category | flops | bytes accessed | tf_op | source)
XLA Modules:
  0.0 269.8 jit_solution(2288781871409935307)
XLA Ops:
  0.0 1.3 slice.190
  1.6 1.3 slice.191
  3.5 2.4 collective-permute-start
  7.5 1.3 maximum_convert_fusion.1
  8.8 11.8 %fusion.204 = bf16[2048,256]{1,0:T(8,128)(2,1)} fusion(f32[2048,262]{1,0:T(8,128)S(1)} %get-tuple-element.288, f32[2048,262]{1,0:T(8,128)S(1)} %get-tuple-element.287, f32[2048]{0:T(1024)S(1)} %bitcast.245, f32[2048]{0:T(1024)S(1)} %bitcast.244, f32[2048]{0:T(1024)S(1)} %bitcast.233, f32[2048]{0:T(1024)S(1)} %bitcast.234, f32[2048]{0:T(1024)S(1)} %bitcast.235, ...), kind=kLoop, calls=%fused_computation.203 | loop fusion | flops 14680064 | bytes 30523392 | tf_op jit(solution)/shard_map/convert_element_type | solution.py:125
  20.6 7.9 %all-to-all-start = ((bf16[8,256,256]{2,1,0:T(8,128)(2,1)}), bf16[8,256,256]{2,1,0:T(8,128)(2,1)S(1)}, u32[]{:S(2)}, u32[]{:S(2)}) async-start(bf16[8,256,256]{2,1,0:T(8,128)(2,1)} %bitcast.27), calls=%async_computation | async-start | bytes 2097152 | tf_op jit(solution)/shard_map/all_to_all | solution.py:126
  29.9 14.0 %all-to-all-done = bf16[8,256,256]{2,1,0:T(8,128)(2,1)S(1)} async-done(((bf16[8,256,256]{2,1,0:T(8,128)(2,1)}), bf16[8,256,256]{2,1,0:T(8,128)(2,1)S(1)}, u32[]{:S(2)}, u32[]{:S(2)}) %all-to-all-start) | async-done | bytes 1048608 | tf_op jit(solution)/shard_map/all_to_all | solution.py:126
  45.0 195.2 %while.12 = (s32[]{:T(128)}, bf16[16,16,2048]{2,1,0:T(8,128)(2,1)}, bf16[16,16,2048]{2,1,0:T(8,128)(2,1)S(1)}, bf16[16,16,2048]{2,1,0:T(8,128)(2,1)}, f32[16,16]{1,0:T(8,128)S(1)}, /*index=5*/s32[]{:T(128)}) while((s32[]{:T(128)}, bf16[16,16,2048]{2,1,0:T(8,128)(2,1)}, bf16[16,16,2048]{2,1,0:T(8,128)(2,1)S(1)}, ...), condition=%wide.region_1.2_spmd.clone.clone, body=%wide.region_0.1_spmd.clone.clone.sunk | while | flops 1256058880 | bytes 17597196 | solution.py:95
  45.1 0.9 dynamic-slice_bitcast_fusion.3
  57.2 0.8 dynamic-slice_bitcast_fusion.3
  69.5 0.8 dynamic-slice_bitcast_fusion.3
  81.6 0.8 dynamic-slice_bitcast_fusion.3
  93.8 0.8 dynamic-slice_bitcast_fusion.3
  106.0 0.8 dynamic-slice_bitcast_fusion.3
  118.2 0.8 dynamic-slice_bitcast_fusion.3
  130.4 0.8 dynamic-slice_bitcast_fusion.3
  142.6 0.8 dynamic-slice_bitcast_fusion.3
  240.2 1.5 copy.29
  241.8 1.2 copy.23
  242.9 4.2 %all-to-all-start.1 = ((bf16[256,8,256]{2,0,1:T(8,128)(2,1)}), bf16[256,8,256]{2,0,1:T(8,128)(2,1)}, u32[]{:S(2)}, u32[]{:S(2)}) async-start(bf16[256,8,256]{2,0,1:T(8,128)(2,1)} %copy.23), calls=%async_computation.1 | async-start | bytes 2097152 | tf_op jit(solution)/shard_map/all_to_all | solution.py:128
  247.2 1.1 copy.19
  248.3 2.0 maximum_convert_fusion
  250.3 12.3 %all-to-all-done.1 = bf16[256,8,256]{2,0,1:T(8,128)(2,1)} async-done(((bf16[256,8,256]{2,0,1:T(8,128)(2,1)}), bf16[256,8,256]{2,0,1:T(8,128)(2,1)}, u32[]{:S(2)}, u32[]{:S(2)}) %all-to-all-start.1) | async-done | bytes 1048608 | tf_op jit(solution)/shard_map/all_to_all | solution.py:128
  262.6 7.2 %fusion.223 = bf16[2048,256]{1,0:T(8,128)(2,1)} fusion(f32[2048,262]{1,0:T(8,128)S(1)} %maximum_convert_fusion, f32[2048]{0:T(1024)S(1)} %bitcast.225, f32[2048]{0:T(1024)S(1)} %bitcast.226, f32[2048]{0:T(1024)S(1)} %bitcast.227, f32[2048]{0:T(1024)S(1)} %bitcast.228, f32[2048]{0:T(1024)S(1)} %bitcast.229, f32[2048]{0:T(1024)S(1)} %bitcast.230, ...), kind=kLoop, calls=%fused_computation.243 | loop fusion | flops 9437184 | bytes 16834560 | tf_op jit(solution)/shard_map/convert_element_type | solution.py:107
  (480 shorter events, 189.1 us)
Async XLA Ops:
  0.0 3.1 %copy-start = (bf16[2048,256]{1,0:T(8,128)(2,1)S(1)}, bf16[2048,256]{1,0:T(8,128)(2,1)}, u32[]{:S(2)}) copy-start(bf16[2048,256]{1,0:T(8,128)(2,1)} %param.10) | copy-start | bytes 3145732
  1.3 4.6 %copy-start.2 = (f32[3,7,2048]{2,1,0:T(8,128)S(1)}, f32[3,7,2048]{2,1,0:T(8,128)}, u32[]{:S(2)}) copy-start(f32[3,7,2048]{2,1,0:T(8,128)} %param.11) | copy-start | bytes 516100
  2.8 4.7 %copy-start.1 = (bf16[2048,256]{1,0:T(8,128)(2,1)S(1)}, bf16[2048,256]{1,0:T(8,128)(2,1)}, u32[]{:S(2)}) copy-start(bf16[2048,256]{1,0:T(8,128)(2,1)} %param.9) | copy-start | bytes 3145732
  3.5 3.3 %collective-permute-start = (bf16[3,2048,6]{1,2,0:T(8,128)(2,1)S(1)}, bf16[3,2048,6]{1,2,0:T(8,128)(2,1)S(1)}, u32[]{:S(2)}, u32[]{:S(2)}) collective-permute-start(bf16[3,2048,6]{1,2,0:T(8,128)(2,1)S(1)} %pad_maximum_fusion), channel_id=1, source_target_pairs={{0,4},{4,8},{8,12},{12,16},{16,20},{20,24},{24,28},{1,5},{5,9},{9,... | collective-permute-start | bytes 221192 | tf_op jit(solution)/shard_map/ppermute | solution.py:13
  20.6 8.5 %copy-start.3 = (f32[1,256]{1,0:T(1,128)S(1)}, f32[1,256]{1,0:T(1,128)}, u32[]{:S(2)}) copy-start(f32[1,256]{1,0:T(1,128)} %param.13) | copy-start | bytes 3076
  20.6 23.3 %all-to-all-start = ((bf16[8,256,256]{2,1,0:T(8,128)(2,1)}), bf16[8,256,256]{2,1,0:T(8,128)(2,1)S(1)}, u32[]{:S(2)}, u32[]{:S(2)}) async-start(bf16[8,256,256]{2,1,0:T(8,128)(2,1)} %bitcast.27), calls=%async_computation | async-start | bytes 2097152 | tf_op jit(solution)/shard_map/all_to_all | solution.py:126
  242.9 19.6 %all-to-all-start.1 = ((bf16[256,8,256]{2,0,1:T(8,128)(2,1)}), bf16[256,8,256]{2,0,1:T(8,128)(2,1)}, u32[]{:S(2)}, u32[]{:S(2)}) async-start(bf16[256,8,256]{2,0,1:T(8,128)(2,1)} %copy.23), calls=%async_computation.1 | async-start | bytes 2097152 | tf_op jit(solution)/shard_map/all_to_all | solution.py:128
where the time goes:
time: 271 us; the launch traced here: 270 us
  matrix products  164 us (61%)
  other arithmetic  35.8 us (13%)
  waiting for transfers between devices  27 us (10%)
  local copies, waits for them, and re-layouts  24.4 us (9%)
  starting transfers between devices  14.6 us (5%)
  loops' own time  3.38 us (1%)
    dot_general x32, matrix products, forward(): jnp.einsum('ckb,bm->ckm', twist_re, sin_cols, precision=HIGH)  20.2 us
    dot_general x32, matrix products, forward(): jnp.einsum('ckb,bm->ckm', twist_im, sin_cols, precision=HIGH)  19.7 us
    dot_general x32, matrix products, forward(): jnp.einsum('ckb,bm->ckm', twist_im, cos_cols, precision=HIGH)  19.5 us
    dot_general x32, matrix products, forward(): jnp.einsum('ckb,bm->ckm', twist_re, cos_cols, precision=HIGH)  19.5 us
    dot_general x64, matrix products, first_section(): jnp.einsum('ka,cab->ckb', table_rest, shaped, preferred_element_type=jnp....  17.9 us
    dot_general x64, matrix products, first_section(): jnp.einsum('ka,cab->ckb', table_head, shaped, preferred_element_type=jnp....  17.5 us
    all_to_all x1, waiting for transfers between devices, local(): lax.all_to_all(gated, 'ctx', split_axis=0, concat_axis=1, tiled=True)  14 us
    while x48, local copies, waits for them, and re-layouts  14 us
  transfers between devices with their start and end apart: 3, of which 3 were waited for; matrix products, arithmetic and copies ran while one was open for 2% of the time, Pallas kernels for 0%

commit v1 on v0

--- a/solution.py
+++ b/solution.py
@@ -5,6 +5,22 @@
 from jax.sharding import PartitionSpec as P
 
 HIGH = lax.Precision.HIGHEST
+
+
+def pairwise_exchange(array, axis, split, join):
+    ways, here = (lax.axis_size(axis), lax.axis_index(axis))
+    width = array.shape[split] // ways
+    shape = list(array.shape)
+    shape[split] = width
+    height = shape[join]
+    shape[join] = height * ways
+    full = jnp.zeros(shape, array.dtype)
+    for mask in range(ways):
+        part = lax.dynamic_slice_in_dim(array, (here ^ mask) * width, width, axis=split)
+        if mask:
+            part = lax.ppermute(part, axis, [(d, d ^ mask) for d in range(ways)])
+        full = lax.dynamic_update_slice_in_dim(full, part, (here ^ mask) * height, axis=join)
+    return full
 
 
 def passed_along(value, axis, by):
@@ -123,7 +139,7 @@
         short_conv(extend_home(keys, 1), short_taps[1], tok_local)
         * short_conv(extend_home(values, 2), short_taps[2], tok_local)
     ).astype(jnp.bfloat16)
-    g_owned = lax.all_to_all(gated, "ctx", split_axis=0, concat_axis=1, tiled=True)
+    g_owned = pairwise_exchange(gated, "ctx", 0, 1)
     outgoing = long_conv(g_owned, long_filter[0], skip_gain[0])
     returned = lax.all_to_all(outgoing, "ctx", split_axis=1, concat_axis=0, tiled=True)
     return gate_product(q_short, returned)

time: 271 us -> 257 us (0.948)
  other arithmetic: 35.8 us -> 25 us
  waiting for transfers between devices: 27 us -> 22.6 us
  starting transfers between devices: 14.6 us -> 17.5 us
    all_to_all x1 -> x0, waiting for transfers between devices: 14 us -> none  [local(): lax.all_to_all(gated, 'ctx', split_axis=0, concat_axis=1, tiled=True)]
    ppermute x0 -> x7, starting transfers between devices: none -> 10.9 us  [pairwise_exchange(): part = lax.ppermute(part, axis, [(d, d ^ mask) for d in range(ways)])]
    dynamic_update_slice x16, other arithmetic: 11.5 us -> 1.36 us  [long_conv(): lax.map(one_block, (gated.reshape(count, block, length), filters.reshape(...]
    ppermute x0 -> x7, waiting for transfers between devices: none -> 9.61 us  [pairwise_exchange(): part = lax.ppermute(part, axis, [(d, d ^ mask) for d in range(ways)])]
    all_to_all x1 -> x0, starting transfers between devices: 7.94 us -> none  [local(): lax.all_to_all(gated, 'ctx', split_axis=0, concat_axis=1, tiled=True)]
  transfers between devices with their start and end apart: 3 -> 9, of which waited for: 3 -> 5; matrix products, arithmetic and copies ran while one was open for 2% -> 2% of each run, Pallas kernels for 0% -> 0%
where the time goes in v1:
time: 257 us; the launch traced here: 256 us
  matrix products  165 us (64%)
  other arithmetic  25 us (10%)
  waiting for transfers between devices  22.6 us (9%)
  local copies, waits for them, and re-layouts  22.4 us (9%)
  starting transfers between devices  17.5 us (7%)
  loops' own time  3.65 us (1%)
    dot_general x32, matrix products, forward(): jnp.einsum('ckb,bm->ckm', twist_re, sin_cols, precision=HIGH)  20.2 us
    dot_general x32, matrix products, forward(): jnp.einsum('ckb,bm->ckm', twist_im, sin_cols, precision=HIGH)  19.8 us
    dot_general x32, matrix products, forward(): jnp.einsum('ckb,bm->ckm', twist_im, cos_cols, precision=HIGH)  19.5 us
    dot_general x32, matrix products, forward(): jnp.einsum('ckb,bm->ckm', twist_re, cos_cols, precision=HIGH)  19.5 us
    dot_general x64, matrix products, first_section(): jnp.einsum('ka,cab->ckb', table_rest, shaped, preferred_element_type=jnp....  17.9 us
    dot_general x64, matrix products, first_section(): jnp.einsum('ka,cab->ckb', table_head, shaped, preferred_element_type=jnp....  17.5 us
    while x48, local copies, waits for them, and re-layouts  14 us
    all_to_all x1, waiting for transfers between devices, local(): lax.all_to_all(outgoing, 'ctx', split_axis=1, concat_axis=0, tiled=True)  12.3 us
  transfers between devices with their start and end apart: 9, of which 5 were waited for; matrix products, arithmetic and copies ran while one was open for 2% of the time, Pallas kernels for 0%

profile of v1, /device:TPU:0, one launch (start us, length us, event | category | flops | bytes accessed | tf_op | source)
XLA Modules:
  0.0 256.0 jit_solution(15116046127427045337)
XLA Ops:
  0.0 1.3 slice.190
  1.6 1.3 slice.191
  3.5 2.4 collective-permute-start
  7.5 1.3 maximum_convert_fusion.1
  8.8 11.3 %fusion.204 = bf16[2048,256]{1,0:T(8,128)(2,1)S(1)} fusion(f32[2048,262]{1,0:T(8,128)S(1)} %get-tuple-element.296, f32[2048,262]{1,0:T(8,128)S(1)} %get-tuple-element.295, f32[2048]{0:T(1024)S(1)} %bitcast.246, f32[2048]{0:T(1024)S(1)} %bitcast.245, f32[2048]{0:T(1024)S(1)} %bitcast.234, f32[2048]{0:T(1024)S(1)} %bitcast.235, f32[2048]{0:T(1024)S(1)} %bitcast.236, ...), kind=kLoop, calls=%fused_computation.203 | loop fusion | flops 14680064 | bytes 30523392 | tf_op jit(solution)/shard_map/convert_element_type | solution.py:141
  20.3 3.4 %collective-permute-start.1 = (bf16[256,256]{1,0:T(8,128)(2,1)S(1)}, bf16[256,256]{1,0:T(8,128)(2,1)S(1)}, u32[]{:S(2)}, u32[]{:S(2)}) collective-permute-start(bf16[256,256]{1,0:T(8,128)(2,1)S(1)} %get-tuple-element.269), channel_id=1, source_target_pairs={{0,4},{4,0},{8,12},{12,8},{16,20},{20,16},{24,28},{28,24},{1,5},{5... | collective-permute-start | bytes 393224 | tf_op jit(solution)/shard_map/ppermute | solution.py:21
  23.7 2.4 collective-permute-start.2
  27.3 2.7 %collective-permute-start.4 = (bf16[256,256]{1,0:T(8,128)(2,1)S(1)}, bf16[256,256]{1,0:T(8,128)(2,1)S(1)}, u32[]{:S(2)}, u32[]{:S(2)}) collective-permute-start(bf16[256,256]{1,0:T(8,128)(2,1)S(1)} %get-tuple-element.266), channel_id=1, source_target_pairs={{0,16},{4,20},{8,24},{12,28},{16,0},{20,4},{24,8},{28,12},{1,17},{... | collective-permute-start | bytes 393224 | tf_op jit(solution)/shard_map/ppermute | solution.py:21
  29.9 1.7 collective-permute-start.6
  32.7 6.6 %collective-permute-done.4 = bf16[256,256]{1,0:T(8,128)(2,1)S(1)} collective-permute-done((bf16[256,256]{1,0:T(8,128)(2,1)S(1)}, bf16[256,256]{1,0:T(8,128)(2,1)S(1)}, u32[]{:S(2)}, u32[]{:S(2)}) %collective-permute-start.4) | collective-permute-done | bytes 131104 | tf_op jit(solution)/shard_map/ppermute | solution.py:21
  39.3 2.7 %collective-permute-done.5 = bf16[256,256]{1,0:T(8,128)(2,1)S(1)} collective-permute-done((bf16[256,256]{1,0:T(8,128)(2,1)S(1)}, bf16[256,256]{1,0:T(8,128)(2,1)S(1)}, u32[]{:S(2)}, u32[]{:S(2)}) %collective-permute-start.5) | collective-permute-done | bytes 131104 | tf_op jit(solution)/shard_map/ppermute | solution.py:21
  42.1 185.5 %while.12 = (s32[]{:T(128)}, bf16[16,16,2048]{2,1,0:T(8,128)(2,1)S(1)}, bf16[16,16,2048]{2,1,0:T(8,128)(2,1)S(1)}, bf16[16,16,2048]{2,1,0:T(8,128)(2,1)}, f32[16,16]{1,0:T(8,128)S(1)}, /*index=5*/s32[]{:T(128)}) while((s32[]{:T(128)}, bf16[16,16,2048]{2,1,0:T(8,128)(2,1)S(1)}, bf16[16,16,2048]{2,1,0:T(8,128)(2,1)S(1)}, ...), condition=%wide.region_1.2_spmd.clone.clone, body=%wide.region_0.1_spmd.clone.clone.sunk | while | flops 1256058880 | bytes 17597136 | solution.py:111
  42.1 0.9 dynamic-slice_bitcast_fusion.3
  53.7 0.9 dynamic-slice_bitcast_fusion.3
  65.3 0.9 dynamic-slice_bitcast_fusion.3
  76.9 0.9 dynamic-slice_bitcast_fusion.3
  181.3 0.9 dynamic-slice_bitcast_fusion.3
  204.5 0.9 dynamic-slice_bitcast_fusion.3
  228.0 1.2 copy.14
  229.1 4.2 %all-to-all-start = ((bf16[256,8,256]{2,0,1:T(8,128)(2,1)}), bf16[256,8,256]{2,0,1:T(8,128)(2,1)}, u32[]{:S(2)}, u32[]{:S(2)}) async-start(bf16[256,8,256]{2,0,1:T(8,128)(2,1)} %copy.14), calls=%async_computation | async-start | bytes 2097152 | tf_op jit(solution)/shard_map/all_to_all | solution.py:144
  233.4 1.1 copy.11
  234.5 2.0 maximum_convert_fusion
  236.5 12.3 %all-to-all-done = bf16[256,8,256]{2,0,1:T(8,128)(2,1)} async-done(((bf16[256,8,256]{2,0,1:T(8,128)(2,1)}), bf16[256,8,256]{2,0,1:T(8,128)(2,1)}, u32[]{:S(2)}, u32[]{:S(2)}) %all-to-all-start) | async-done | bytes 1048608 | tf_op jit(solution)/shard_map/all_to_all | solution.py:144
  248.8 7.2 %fusion.223 = bf16[2048,256]{1,0:T(8,128)(2,1)} fusion(f32[2048,262]{1,0:T(8,128)S(1)} %maximum_convert_fusion, f32[2048]{0:T(1024)S(1)} %bitcast.226, f32[2048]{0:T(1024)S(1)} %bitcast.227, f32[2048]{0:T(1024)S(1)} %bitcast.228, f32[2048]{0:T(1024)S(1)} %bitcast.229, f32[2048]{0:T(1024)S(1)} %bitcast.230, f32[2048]{0:T(1024)S(1)} %bitcast.231, ...), kind=kLoop, calls=%fused_computation.243 | loop fusion | flops 9437184 | bytes 16834560 | tf_op jit(solution)/shard_map/convert_element_type | solution.py:123
  (499 shorter events, 182.0 us)
Async XLA Ops:
  0.0 3.1 %copy-start = (bf16[2048,256]{1,0:T(8,128)(2,1)S(1)}, bf16[2048,256]{1,0:T(8,128)(2,1)}, u32[]{:S(2)}) copy-start(bf16[2048,256]{1,0:T(8,128)(2,1)} %param.10) | copy-start | bytes 3145732
  1.3 4.6 %copy-start.2 = (f32[3,7,2048]{2,1,0:T(8,128)S(1)}, f32[3,7,2048]{2,1,0:T(8,128)}, u32[]{:S(2)}) copy-start(f32[3,7,2048]{2,1,0:T(8,128)} %param.11) | copy-start | bytes 516100
  2.8 4.7 %copy-start.1 = (bf16[2048,256]{1,0:T(8,128)(2,1)S(1)}, bf16[2048,256]{1,0:T(8,128)(2,1)}, u32[]{:S(2)}) copy-start(bf16[2048,256]{1,0:T(8,128)(2,1)} %param.9) | copy-start | bytes 3145732
  3.5 3.3 %collective-permute-start = (bf16[3,2048,6]{1,2,0:T(8,128)(2,1)S(1)}, bf16[3,2048,6]{1,2,0:T(8,128)(2,1)S(1)}, u32[]{:S(2)}, u32[]{:S(2)}) collective-permute-start(bf16[3,2048,6]{1,2,0:T(8,128)(2,1)S(1)} %pad_maximum_fusion), channel_id=1, source_target_pairs={{0,4},{4,8},{8,12},{12,16},{16,20},{20,24},{24,28},{1,5},{5,9},{9,... | collective-permute-start | bytes 221192 | tf_op jit(solution)/shard_map/ppermute | solution.py:29
  20.1 6.5 %copy-start.3 = (f32[1,256]{1,0:T(1,128)S(1)}, f32[1,256]{1,0:T(1,128)}, u32[]{:S(2)}) copy-start(f32[1,256]{1,0:T(1,128)} %param.13) | copy-start | bytes 3076
  20.3 9.6 %collective-permute-start.1 = (bf16[256,256]{1,0:T(8,128)(2,1)S(1)}, bf16[256,256]{1,0:T(8,128)(2,1)S(1)}, u32[]{:S(2)}, u32[]{:S(2)}) collective-permute-start(bf16[256,256]{1,0:T(8,128)(2,1)S(1)} %get-tuple-element.269), channel_id=1, source_target_pairs={{0,4},{4,0},{8,12},{12,8},{16,20},{20,16},{24,28},{28,24},{1,5},{5... | collective-permute-start | bytes 393224 | tf_op jit(solution)/shard_map/ppermute | solution.py:21
  23.7 8.0 %collective-permute-start.2 = (bf16[256,256]{1,0:T(8,128)(2,1)S(1)}, bf16[256,256]{1,0:T(8,128)(2,1)S(1)}, u32[]{:S(2)}, u32[]{:S(2)}) collective-permute-start(bf16[256,256]{1,0:T(8,128)(2,1)S(1)} %get-tuple-element.268), channel_id=1, source_target_pairs={{0,8},{4,12},{8,0},{12,4},{16,24},{20,28},{24,16},{28,20},{1,9},{5... | collective-permute-start | bytes 393224 | tf_op jit(solution)/shard_map/ppermute | solution.py:21
  27.2 5.5 %collective-permute-start.3 = (bf16[256,256]{1,0:T(8,128)(2,1)S(1)}, bf16[256,256]{1,0:T(8,128)(2,1)S(1)}, u32[]{:S(2)}, u32[]{:S(2)}) collective-permute-start(bf16[256,256]{1,0:T(8,128)(2,1)S(1)} %get-tuple-element.267), channel_id=1, source_target_pairs={{0,12},{4,8},{8,4},{12,0},{16,28},{20,24},{24,20},{28,16},{1,13},{... | collective-permute-start | bytes 393224 | tf_op jit(solution)/shard_map/ppermute | solution.py:21
  27.3 12.0 %collective-permute-start.4 = (bf16[256,256]{1,0:T(8,128)(2,1)S(1)}, bf16[256,256]{1,0:T(8,128)(2,1)S(1)}, u32[]{:S(2)}, u32[]{:S(2)}) collective-permute-start(bf16[256,256]{1,0:T(8,128)(2,1)S(1)} %get-tuple-element.266), channel_id=1, source_target_pairs={{0,16},{4,20},{8,24},{12,28},{16,0},{20,4},{24,8},{28,12},{1,17},{... | collective-permute-start | bytes 393224 | tf_op jit(solution)/shard_map/ppermute | solution.py:21
  29.9 12.1 %collective-permute-start.5 = (bf16[256,256]{1,0:T(8,128)(2,1)S(1)}, bf16[256,256]{1,0:T(8,128)(2,1)S(1)}, u32[]{:S(2)}, u32[]{:S(2)}) collective-permute-start(bf16[256,256]{1,0:T(8,128)(2,1)S(1)} %get-tuple-element.265), channel_id=1, source_target_pairs={{0,20},{4,16},{8,28},{12,24},{16,4},{20,0},{24,12},{28,8},{1,21},{... | collective-permute-start | bytes 393224 | tf_op jit(solution)/shard_map/ppermute | solution.py:21
  29.9 12.1 %collective-permute-start.6 = (bf16[256,256]{1,0:T(8,128)(2,1)S(1)}, bf16[256,256]{1,0:T(8,128)(2,1)S(1)}, u32[]{:S(2)}, u32[]{:S(2)}) collective-permute-start(bf16[256,256]{1,0:T(8,128)(2,1)S(1)} %get-tuple-element.264), channel_id=1, source_target_pairs={{0,24},{4,28},{8,16},{12,20},{16,8},{20,12},{24,0},{28,4},{1,25},{... | collective-permute-start | bytes 393224 | tf_op jit(solution)/shard_map/ppermute | solution.py:21
  31.7 10.4 %collective-permute-start.7 = (bf16[256,256]{1,0:T(8,128)(2,1)S(1)}, bf16[256,256]{1,0:T(8,128)(2,1)S(1)}, u32[]{:S(2)}, u32[]{:S(2)}) collective-permute-start(bf16[256,256]{1,0:T(8,128)(2,1)S(1)} %get-tuple-element.263), channel_id=1, source_target_pairs={{0,28},{4,24},{8,20},{12,16},{16,12},{20,8},{24,4},{28,0},{1,29},{... | collective-permute-start | bytes 393224 | tf_op jit(solution)/shard_map/ppermute | solution.py:21
  229.1 19.6 %all-to-all-start = ((bf16[256,8,256]{2,0,1:T(8,128)(2,1)}), bf16[256,8,256]{2,0,1:T(8,128)(2,1)}, u32[]{:S(2)}, u32[]{:S(2)}) async-start(bf16[256,8,256]{2,0,1:T(8,128)(2,1)} %copy.14), calls=%async_computation | async-start | bytes 2097152 | tf_op jit(solution)/shard_map/all_to_all | solution.py:144
